TPU v7x, 128 devices: a whole 4x4x4 slice. The times are simulated.
128 devices in a mesh: bond: 8 (over x, core), op: 16 (over y, z).
Axes of the slice: x: 4, y: 4, z: 4, core: 2. Of those that a mesh axis runs over, the one named last changes fastest.
Arguments:
- wave_slab: bfloat16 [8192, 8192], P('op', 'bond'), may hold values from -6 to 6
- left_blocks: bfloat16 [32, 16, 2, 128, 128], P('op'), may hold values from -0.375 to 0.375
- right_blocks: bfloat16 [32, 64, 2, 128, 128], P('op'), may hold values from -0.0625 to 0.0625
- sector_size: int32 [64], replicated, may hold values from 1 to 128
- left_pairs: int32 [32, 16, 2], P('op'), may hold values from 0 to 63
- right_pairs: int32 [32, 64, 2], P('op'), may hold values from 0 to 63
Outputs:
- applied: float32 [2048, 8192], P('bond', 'op')
All inputs are finite; a program needn't handle non-finite values.
Results may differ from a plain program's by a relative error of at most 0.0029.
Values may be sent and summed in bfloat16 or wider, within the bound.
No kernel may reach another device: no remote copies, remote signals or barrier semaphores. Data moves between devices by JAX's collectives and lax.ppermute only.
A program may use at most 128 MiB of HBM per device.

v0:
```python
import jax
import jax.numpy as jnp
from jax import lax
from jax.sharding import PartitionSpec as P

TILE = 128


def live_mask(sector_size):
    states = jnp.arange(TILE, dtype=jnp.int32)
    return (states[None, :] < sector_size[:, None]).astype(jnp.float32).reshape(-1)


def on_device(wave_slab, left_blocks, right_blocks, sector_size, left_pairs, right_pairs):
    live = live_mask(sector_size)
    local_rows = wave_slab.shape[0]
    strip = wave_slab.shape[1]
    row_live = lax.dynamic_slice_in_dim(live, lax.axis_index("op") * local_rows, local_rows)
    col_live = lax.dynamic_slice_in_dim(live, lax.axis_index("bond") * strip, strip)
    masked = (wave_slab.astype(jnp.float32) * row_live[:, None] * col_live[None, :]).astype(
        jnp.bfloat16
    )
    whole = lax.all_gather(masked, "op", axis=0, tiled=True)
    full_width = whole.shape[0]
    sector_count = full_width // TILE
    sectors = whole.reshape(sector_count, TILE, strip)
    term_count = left_blocks.shape[0]
    middles = []
    for term_idx in range(term_count):
        picked = sectors[left_pairs[term_idx]]
        middle = jnp.einsum(
            "ipxy,ipys->ixs", left_blocks[term_idx], picked, preferred_element_type=jnp.float32
        )
        middles.append(middle.astype(jnp.bfloat16).reshape(-1, strip))
    stacked = jnp.stack(middles, 0)
    bond_count = lax.axis_size("bond")
    slab_rows = stacked.shape[1]
    share_rows = slab_rows // bond_count
    blocked = stacked.reshape(term_count, bond_count, share_rows, strip)
    arrived = lax.all_to_all(blocked, "bond", split_axis=1, concat_axis=3, tiled=True)
    row_count = arrived.shape[2]
    total = jnp.zeros((row_count, sector_count, TILE), jnp.float32)
    for term_idx in range(term_count):
        split_cols = arrived[term_idx, 0].reshape(row_count, sector_count, TILE)
        chosen = split_cols[:, right_pairs[term_idx]]
        total = total + jnp.einsum(
            "rjpy,jpyz->rjz", chosen, right_blocks[term_idx], preferred_element_type=jnp.float32
        )
    partial_value = total.reshape(row_count, full_width)
    summed = lax.psum_scatter(partial_value, "op", scatter_dimension=1, tiled=True)
    out_cols = summed.shape[1]
    out_row_live = lax.dynamic_slice_in_dim(live, lax.axis_index("bond") * share_rows, share_rows)
    out_col_live = lax.dynamic_slice_in_dim(live, lax.axis_index("op") * out_cols, out_cols)
    return summed * out_row_live[:, None] * out_col_live[None, :]


def solution(mesh):
    placed = (
        P("op", "bond"),
        P("op", None, None, None, None),
        P("op", None, None, None, None),
        P(),
        P("op", None, None),
        P("op", None, None),
    )
    return jax.shard_map(
        on_device, mesh=mesh, in_specs=placed, out_specs=P("bond", "op"), check_vma=False
    )
```

profile of v0, /device:TPU:0, one launch (start us, length us, event | category | flops | bytes accessed | tf_op | source)
XLA Modules:
  0.0 447.6 jit_solution(14537597451842649991)
XLA Ops:
  6.5 0.0 all-gather.2.cloned.1.call-start
  6.5 0.7 convert_bitcast_fusion
  7.3 0.1 dynamic_slice.10
  7.4 2.5 multiply_convert_fusion
  9.9 0.0 all-gather.2.cloned.1.call-update
  9.9 0.7 compare_select_fusion.3
  10.6 0.1 copy.25
  10.7 0.1 reshape.143
  10.8 0.1 copy.26
  10.9 0.1 reshape.151
  11.0 112.9 %all-gather.2.cloned.1.call-done = bf16[8192,1024]{1,0:T(8,128)(2,1)} async-done(((bf16[512,1024]{1,0:T(8,128)(2,1)}), bf16[8192,1024]{1,0:T(8,128)(2,1)}) %all-gather.2.cloned.1.call-update) | async-done | bytes 16777232 | tf_op jit(solution)/shard_map/all_gather | solution.py:23
  123.9 0.0 copy-start
  123.9 10.9 %gather_fusion = bf16[32,128,1024]{2,1,0:T(8,128)(2,1)} fusion(bf16[64,128,1024]{2,1,0:T(8,128)(2,1)} %bitcast.83, s32[1024]{0:T(1024)S(1)} %pad_clamp_fusion.3), kind=kCustom, calls=%fused_computation | custom fusion | bytes 16777344 | tf_op jit(solution)/shard_map/gather | solution.py:30
  134.8 0.0 copy-done
  134.8 6.6 %bitcast_convert_fusion.1 = bf16[16,1024,128]{1,2,0:T(8,128)(2,1)} fusion(bf16[16,2,128,1024]{3,2,1,0:T(8,128)(2,1)} %bitcast.76, bf16[2,16,2,128,128]{4,3,2,1,0:T(8,128)(2,1)S(1)} %copy-done), kind=kOutput, calls=%fused_computation.7 | convolution fusion | flops 1075838976 | bytes 13631488 | tf_op jit(solution)/shard_map/ipxy,ipys->ixs/dot_general | solution.py:31
  141.4 6.4 %copy.27 = bf16[1,8,256,1024]{2,3,0,1:T(8,128)(2,1)} copy(bf16[1,8,256,1024]{3,2,1,0:T(8,128)(2,1)} %bitcast.81) | data formatting | bytes 8388608 | tf_op jit(solution)/shard_map/stack | solution.py:35
  147.8 10.8 %gather_fusion.1 = bf16[32,128,1024]{2,1,0:T(8,128)(2,1)} fusion(bf16[64,128,1024]{2,1,0:T(8,128)(2,1)} %bitcast.84, s32[1024]{0:T(1024)S(1)} %pad_clamp_fusion.2), kind=kCustom, calls=%fused_computation.1 | custom fusion | bytes 16777344 | tf_op jit(solution)/shard_map/gather | solution.py:30
  158.6 6.6 %bitcast_convert_fusion = bf16[16,1024,128]{1,2,0:T(8,128)(2,1)} fusion(bf16[16,2,128,1024]{3,2,1,0:T(8,128)(2,1)} %bitcast.75, bf16[2,16,2,128,128]{4,3,2,1,0:T(8,128)(2,1)S(1)} %copy-done), kind=kOutput, calls=%fused_computation.6 | convolution fusion | flops 1075838976 | bytes 13631488 | tf_op jit(solution)/shard_map/ipxy,ipys->ixs/dot_general | solution.py:31
  165.2 6.5 %copy.28 = bf16[1,8,256,1024]{2,3,0,1:T(8,128)(2,1)} copy(bf16[1,8,256,1024]{3,2,1,0:T(8,128)(2,1)} %bitcast.82) | data formatting | bytes 8388608 | tf_op jit(solution)/shard_map/stack | solution.py:35
  171.7 7.5 %pad_maximum_fusion = bf16[2,8,256,1024]{2,3,0,1:T(8,128)(2,1)} fusion(bf16[1,8,256,1024]{2,3,0,1:T(8,128)(2,1)} %copy.28, bf16[1,8,256,1024]{2,3,0,1:T(8,128)(2,1)} %copy.27), kind=kLoop, calls=%fused_computation.4 | loop fusion | flops 4194304 | bytes 16777216 | tf_op jit(solution)/shard_map/stack | solution.py:35
  179.1 0.0 copy-start.1
  179.1 5.2 %all-to-all-start = ((bf16[2,8,256,1024]{2,3,0,1:T(8,128)(2,1)}), bf16[2,8,256,1024]{2,3,0,1:T(8,128)(2,1)}, u32[]{:S(2)}, u32[]{:S(2)}) async-start(bf16[2,8,256,1024]{2,3,0,1:T(8,128)(2,1)} %pad_maximum_fusion), calls=%async_computation | async-start | bytes 16777216 | tf_op jit(solution)/shard_map/all_to_all | solution.py:40
  184.3 0.2 reduce-scatter.2.cloned.1.call-start
  184.5 0.0 copy-done.1
  184.5 0.1 copy.33
  184.6 0.1 reshape.167
  184.8 0.1 copy.30
  184.9 0.1 reshape.159
  185.0 93.8 %all-to-all-done = bf16[2,8,256,1024]{2,3,0,1:T(8,128)(2,1)} async-done(((bf16[2,8,256,1024]{2,3,0,1:T(8,128)(2,1)}), bf16[2,8,256,1024]{2,3,0,1:T(8,128)(2,1)}, u32[]{:S(2)}, u32[]{:S(2)}) %all-to-all-start) | async-done | bytes 8388640 | tf_op jit(solution)/shard_map/all_to_all | solution.py:40
  278.9 7.3 %copy.44 = bf16[2,8,256,1024]{2,3,1,0:T(8,128)(2,1)} copy(bf16[2,8,256,1024]{2,3,0,1:T(8,128)(2,1)} %all-to-all-done) | data formatting | bytes 16777216 | tf_op jit(solution)/shard_map/all_to_all | solution.py:40
  286.2 5.7 %fusion.12 = (bf16[1,1,256,8,1024]{2,4,3,1,0:T(8,128)(2,1)}, bf16[1,1,256,8,1024]{2,4,3,1,0:T(8,128)(2,1)}) fusion(bf16[2,1,256,8,1024]{2,4,3,1,0:T(8,128)(2,1)} %bitcast.79), kind=kLoop, calls=%fused_computation.31 | loop fusion | bytes 16777216 | tf_op jit(solution)/shard_map/slice | solution.py:44
  291.9 6.4 %copy.34 = bf16[256,64,128]{2,0,1:T(8,128)(2,1)} copy(bf16[256,64,128]{0,2,1:T(8,128)(2,1)} %bitcast.86) | data formatting | bytes 8388608 | tf_op jit(solution)/shard_map/reshape;squeeze | solution.py:44
  298.3 6.3 %copy.31 = bf16[256,64,128]{2,0,1:T(8,128)(2,1)} copy(bf16[256,64,128]{0,2,1:T(8,128)(2,1)} %bitcast.85) | data formatting | bytes 8388608 | tf_op jit(solution)/shard_map/reshape;squeeze | solution.py:44
  304.6 8.8 %gather_fusion.3 = bf16[128,256,128]{2,1,0:T(8,128)(2,1)} fusion(bf16[256,64,128]{2,0,1:T(8,128)(2,1)} %copy.34, s32[1024]{0:T(1024)S(1)} %pad_clamp_fusion), kind=kCustom, calls=%fused_computation.3 | custom fusion | bytes 16777728 | tf_op jit(solution)/shard_map/gather | solution.py:45
  313.4 10.7 %fusion = f32[64,256,128,1]{1,2,3,0:T(8,128)} fusion(bf16[256,64,2,128]{3,0,2,1:T(8,128)(2,1)} %bitcast.80, bf16[2,64,2,128,128]{4,3,2,1,0:T(8,128)(2,1)} %param.8), kind=kOutput, calls=%fused_computation.9 | convolution fusion | flops 1073741824 | bytes 20971520 | tf_op jit(solution)/shard_map/rjpy,jpyz->rjz/dot_general | solution.py:46
  324.1 8.8 %gather_fusion.2 = bf16[128,256,128]{2,1,0:T(8,128)(2,1)} fusion(bf16[256,64,128]{2,0,1:T(8,128)(2,1)} %copy.31, s32[1024]{0:T(1024)S(1)} %pad_clamp_fusion.1), kind=kCustom, calls=%fused_computation.2 | custom fusion | bytes 16777728 | tf_op jit(solution)/shard_map/gather | solution.py:45
  332.8 13.2 %bitcast_add_fusion = f32[64,256,128]{1,2,0:T(8,128)} fusion(f32[64,256,128,1]{1,2,3,0:T(8,128)} %fusion, bf16[256,64,2,128]{3,0,2,1:T(8,128)(2,1)} %bitcast.77, bf16[2,64,2,128,128]{4,3,2,1,0:T(8,128)(2,1)} %param.8), kind=kOutput, calls=%fused_computation.5 | convolution fusion | flops 1075838976 | bytes 29360128 | tf_op jit(solution)/shard_map/rjpy,jpyz->rjz/dot_general | solution.py:46
  346.0 8.9 %copy.36 = f32[256,8192]{1,0:T(8,128)} copy(f32[256,8192]{0,1:T(8,128)} %bitcast.78) | data formatting | bytes 16777216 | tf_op jit(solution)/shard_map/reshape | solution.py:49
  354.9 0.0 reduce-scatter.2.cloned.1.call-update
  354.9 0.1 dynamic_slice.12
  355.0 83.9 %reduce-scatter.2.cloned.1.call-done = f32[256,512]{1,0:T(8,128)} async-done(((f32[256,8192]{1,0:T(8,128)}), f32[256,512]{1,0:T(8,128)}) %reduce-scatter.2.cloned.1.call-update) | async-done | bytes 524304 | tf_op jit(solution)/shard_map/reduce_scatter | solution.py:50
  438.9 1.9 multiply_multiply_fusion
  (6 shorter events, 0.0 us)
Async XLA Ops:
  6.5 117.3 %all-gather.2.cloned.1.call-start = ((), (), s32[]{:S(2)}) async-start(), calls=%async_computation.2 | async-start | bytes 17825792 | tf_op jit(solution)/shard_map/all_gather | solution.py:23
  123.9 10.9 %copy-start = (bf16[2,16,2,128,128]{4,3,2,1,0:T(8,128)(2,1)S(1)}, bf16[2,16,2,128,128]{4,3,2,1,0:T(8,128)(2,1)}, u32[]{:S(2)}) copy-start(bf16[2,16,2,128,128]{4,3,2,1,0:T(8,128)(2,1)} %param.7) | copy-start | bytes 6291460
  179.1 5.4 %copy-start.1 = (s32[2,64,2]{1,2,0:T(2,128)S(1)}, s32[2,64,2]{1,2,0:T(2,128)}, u32[]{:S(2)}) copy-start(s32[2,64,2]{1,2,0:T(2,128)} %param.11) | copy-start | bytes 3076
  179.1 99.8 %all-to-all-start = ((bf16[2,8,256,1024]{2,3,0,1:T(8,128)(2,1)}), bf16[2,8,256,1024]{2,3,0,1:T(8,128)(2,1)}, u32[]{:S(2)}, u32[]{:S(2)}) async-start(bf16[2,8,256,1024]{2,3,0,1:T(8,128)(2,1)} %pad_maximum_fusion), calls=%async_computation | async-start | bytes 16777216 | tf_op jit(solution)/shard_map/all_to_all | solution.py:40
  184.3 254.6 %reduce-scatter.2.cloned.1.call-start = ((), (), s32[]{:S(2)}) async-start(), calls=%async_computation.3 | async-start | bytes 8912896 | tf_op jit(solution)/shard_map/reduce_scatter | solution.py:50
Sparse Core Ops, SparseCore 0:
  10.0 113.8 all-gather.1
  355.0 83.7 reduce-scatter.1
where the time goes:
time: 449 us; the launch traced here: 448 us
  waiting for transfers between devices  291 us (65%)
  local copies, waits for them, and re-layouts  87.8 us (20%)
  matrix products  37 us (8%)
  between operations  13.5 us (3%)
  other arithmetic  13.4 us (3%)
  starting transfers between devices  5.4 us (1%)
    all_gather x1, waiting for transfers between devices, on_device(): whole = lax.all_gather(masked, 'op', axis=0, tiled=True)  113 us
    all_to_all x1, waiting for transfers between devices, on_device(): lax.all_to_all(blocked, 'bond', split_axis=1, concat_axis=3, tiled=True)  93.8 us
    reduce_scatter x1, waiting for transfers between devices, on_device(): lax.psum_scatter(partial_value, 'op', scatter_dimension=1, tiled=True)  83.9 us
    dot_general x2, matrix products, on_device(): jnp.einsum('rjpy,jpyz->rjz', chosen, right_blocks[term_idx], preferred_el...  23.8 us
    gather x2, local copies, waits for them, and re-layouts, on_device(): picked = sectors[left_pairs[term_idx]]  21.7 us
    gather x2, local copies, waits for them, and re-layouts, on_device(): chosen = split_cols[:, right_pairs[term_idx]]  17.6 us
    dot_general x2, matrix products, on_device(): jnp.einsum('ipxy,ipys->ixs', left_blocks[term_idx], picked, preferred_ele...  13.2 us
    another operation x2, local copies, waits for them, and re-layouts, on_device(): stacked = jnp.stack(middles, 0)  12.9 us
  transfers between devices with their start and end apart: 3, of which 3 were waited for; matrix products, arithmetic and copies ran while one was open for 0% of the time, Pallas kernels for 0%

commit v1 on v0

--- a/solution.py
+++ b/solution.py
@@ -20,7 +20,9 @@
     masked = (wave_slab.astype(jnp.float32) * row_live[:, None] * col_live[None, :]).astype(
         jnp.bfloat16
     )
-    whole = lax.all_gather(masked, "op", axis=0, tiled=True)
+    whole = jnp.concatenate(
+        lax.all_to_all(jnp.stack([masked] * lax.axis_size("op")), "op", 0, 0), axis=0
+    )
     full_width = whole.shape[0]
     sector_count = full_width // TILE
     sectors = whole.reshape(sector_count, TILE, strip)

time: 449 us -> 648 us (1.44)
  waiting for transfers between devices: 291 us -> 477 us
  starting transfers between devices: 5.4 us -> 13.7 us
    all_to_all x0 -> x1, waiting for transfers between devices: none -> 293 us  [on_device(): lax.all_to_all(jnp.stack([masked] * lax.axis_size('op')), 'op', 0, 0)]
    all_gather x1 -> x0, waiting for transfers between devices: 113 us -> none  [on_device(): whole = lax.all_gather(masked, 'op', axis=0, tiled=True)]
    all_to_all x0 -> x1, starting transfers between devices: none -> 8.34 us  [on_device(): lax.all_to_all(jnp.stack([masked] * lax.axis_size('op')), 'op', 0, 0)]
where the time goes in v1:
time: 648 us; the launch traced here: 646 us
  waiting for transfers between devices  477 us (74%)
  local copies, waits for them, and re-layouts  93.8 us (14%)
  matrix products  37 us (6%)
  starting transfers between devices  13.7 us (2%)
  between operations  13.5 us (2%)
  other arithmetic  11.7 us (2%)
    all_to_all x1, waiting for transfers between devices, on_device(): lax.all_to_all(jnp.stack([masked] * lax.axis_size('op')), 'op', 0, 0)  293 us
    all_to_all x1, waiting for transfers between devices, on_device(): lax.all_to_all(blocked, 'bond', split_axis=1, concat_axis=3, tiled=True)  93.8 us
    reduce_scatter x1, waiting for transfers between devices, on_device(): lax.psum_scatter(partial_value, 'op', scatter_dimension=1, tiled=True)  89.2 us
    dot_general x2, matrix products, on_device(): jnp.einsum('rjpy,jpyz->rjz', chosen, right_blocks[term_idx], preferred_el...  23.8 us
    gather x2, local copies, waits for them, and re-layouts, on_device(): picked = sectors[left_pairs[term_idx]]  21.7 us
    gather x2, local copies, waits for them, and re-layouts, on_device(): chosen = split_cols[:, right_pairs[term_idx]]  17.6 us
    dot_general x2, matrix products, on_device(): jnp.einsum('ipxy,ipys->ixs', left_blocks[term_idx], picked, preferred_ele...  13.2 us
  transfers between devices with their start and end apart: 3, of which 3 were waited for; matrix products, arithmetic and copies ran while one was open for 0% of the time, Pallas kernels for 0%

profile of v1, /device:TPU:0, one launch (start us, length us, event | category | flops | bytes accessed | tf_op | source)
XLA Modules:
  0.0 646.4 jit_solution(1902881723506891156)
XLA Ops:
  6.5 0.7 convert_bitcast_fusion
  7.3 0.1 dynamic_slice.10
  7.3 1.5 multiply_convert_fusion
  8.9 6.0 stack.8
  14.9 0.0 copy-start.1
  14.9 8.3 %all-to-all-start = ((bf16[16,512,1024]{2,1,0:T(8,128)(2,1)}), bf16[16,512,1024]{2,1,0:T(8,128)(2,1)}, u32[]{:S(2)}, u32[]{:S(2)}) async-start(bf16[16,512,1024]{2,1,0:T(8,128)(2,1)} %stack.8), calls=%async_computation | async-start | bytes 33554432 | tf_op jit(solution)/shard_map/all_to_all | solution.py:24
  23.3 0.0 copy-done.1
  23.3 0.1 copy.25
  23.4 0.1 reshape.141
  23.5 0.1 copy.26
  23.5 0.1 reshape.149
  23.7 293.5 %all-to-all-done = bf16[16,512,1024]{2,1,0:T(8,128)(2,1)} async-done(((bf16[16,512,1024]{2,1,0:T(8,128)(2,1)}), bf16[16,512,1024]{2,1,0:T(8,128)(2,1)}, u32[]{:S(2)}, u32[]{:S(2)}) %all-to-all-start) | async-done | bytes 16777248 | tf_op jit(solution)/shard_map/all_to_all | solution.py:24
  317.2 10.8 %gather_fusion.1 = bf16[32,128,1024]{2,1,0:T(8,128)(2,1)} fusion(bf16[64,128,1024]{2,1,0:T(8,128)(2,1)} %bitcast.1, s32[1024]{0:T(1024)S(1)} %pad_clamp_fusion.2), kind=kCustom, calls=%fused_computation.1 | custom fusion | bytes 16777344 | tf_op jit(solution)/shard_map/gather | solution.py:32
  327.9 0.0 copy-start
  327.9 10.9 %gather_fusion = bf16[32,128,1024]{2,1,0:T(8,128)(2,1)} fusion(bf16[64,128,1024]{2,1,0:T(8,128)(2,1)} %bitcast.1, s32[1024]{0:T(1024)S(1)} %pad_clamp_fusion.3), kind=kCustom, calls=%fused_computation | custom fusion | bytes 16777344 | tf_op jit(solution)/shard_map/gather | solution.py:32
  338.9 0.0 copy-done
  338.9 6.6 %bitcast_convert_fusion.1 = bf16[16,1024,128]{1,2,0:T(8,128)(2,1)} fusion(bf16[16,2,128,1024]{3,2,1,0:T(8,128)(2,1)} %bitcast.76, bf16[2,16,2,128,128]{4,3,2,1,0:T(8,128)(2,1)S(1)} %copy-done), kind=kOutput, calls=%fused_computation.7 | convolution fusion | flops 1075838976 | bytes 13631488 | tf_op jit(solution)/shard_map/ipxy,ipys->ixs/dot_general | solution.py:33
  345.5 6.5 copy.27
  351.9 6.6 %bitcast_convert_fusion = bf16[16,1024,128]{1,2,0:T(8,128)(2,1)} fusion(bf16[16,2,128,1024]{3,2,1,0:T(8,128)(2,1)} %bitcast.75, bf16[2,16,2,128,128]{4,3,2,1,0:T(8,128)(2,1)S(1)} %copy-done), kind=kOutput, calls=%fused_computation.6 | convolution fusion | flops 1075838976 | bytes 13631488 | tf_op jit(solution)/shard_map/ipxy,ipys->ixs/dot_general | solution.py:33
  358.5 6.5 copy.28
  365.0 7.5 %pad_maximum_fusion = bf16[2,8,256,1024]{2,3,0,1:T(8,128)(2,1)} fusion(bf16[1,8,256,1024]{2,3,0,1:T(8,128)(2,1)} %copy.28, bf16[1,8,256,1024]{2,3,0,1:T(8,128)(2,1)} %copy.27), kind=kLoop, calls=%fused_computation.4 | loop fusion | flops 4194304 | bytes 16777216 | tf_op jit(solution)/shard_map/stack | solution.py:37
  372.4 0.0 copy-start.2
  372.4 5.2 all-to-all-start.1
  377.6 0.2 reduce-scatter.2.cloned.1.call-start
  377.8 0.0 copy-done.2
  377.9 0.1 copy.30
  378.0 0.1 reshape.157
  378.1 0.1 copy.33
  378.2 0.1 reshape.165
  378.4 93.8 %all-to-all-done.1 = bf16[2,8,256,1024]{2,3,0,1:T(8,128)(2,1)} async-done(((bf16[2,8,256,1024]{2,3,0,1:T(8,128)(2,1)}), bf16[2,8,256,1024]{2,3,0,1:T(8,128)(2,1)}, u32[]{:S(2)}, u32[]{:S(2)}) %all-to-all-start.1) | async-done | bytes 8388640 | tf_op jit(solution)/shard_map/all_to_all | solution.py:42
  472.2 7.3 %copy.44 = bf16[2,8,256,1024]{2,3,1,0:T(8,128)(2,1)} copy(bf16[2,8,256,1024]{2,3,0,1:T(8,128)(2,1)} %all-to-all-done.1) | data formatting | bytes 16777216 | tf_op jit(solution)/shard_map/all_to_all | solution.py:42
  479.5 5.7 fusion.12
  485.2 6.3 copy.31
  491.6 6.4 copy.34
  497.9 8.8 %gather_fusion.3 = bf16[128,256,128]{2,1,0:T(8,128)(2,1)} fusion(bf16[256,64,128]{2,0,1:T(8,128)(2,1)} %copy.34, s32[1024]{0:T(1024)S(1)} %pad_clamp_fusion), kind=kCustom, calls=%fused_computation.3 | custom fusion | bytes 16777728 | tf_op jit(solution)/shard_map/gather | solution.py:47
  506.7 10.7 %fusion = f32[64,256,128,1]{1,2,3,0:T(8,128)} fusion(bf16[256,64,2,128]{3,0,2,1:T(8,128)(2,1)} %bitcast.80, bf16[2,64,2,128,128]{4,3,2,1,0:T(8,128)(2,1)} %param.8), kind=kOutput, calls=%fused_computation.9 | convolution fusion | flops 1073741824 | bytes 20971520 | tf_op jit(solution)/shard_map/rjpy,jpyz->rjz/dot_general | solution.py:48
  517.4 8.8 %gather_fusion.2 = bf16[128,256,128]{2,1,0:T(8,128)(2,1)} fusion(bf16[256,64,128]{2,0,1:T(8,128)(2,1)} %copy.31, s32[1024]{0:T(1024)S(1)} %pad_clamp_fusion.1), kind=kCustom, calls=%fused_computation.2 | custom fusion | bytes 16777728 | tf_op jit(solution)/shard_map/gather | solution.py:47
  526.2 13.2 %bitcast_add_fusion = f32[64,256,128]{1,2,0:T(8,128)} fusion(f32[64,256,128,1]{1,2,3,0:T(8,128)} %fusion, bf16[256,64,2,128]{3,0,2,1:T(8,128)(2,1)} %bitcast.77, bf16[2,64,2,128,128]{4,3,2,1,0:T(8,128)(2,1)} %param.8), kind=kOutput, calls=%fused_computation.5 | convolution fusion | flops 1075838976 | bytes 29360128 | tf_op jit(solution)/shard_map/rjpy,jpyz->rjz/dot_general | solution.py:48
  539.3 8.9 %copy.36 = f32[256,8192]{1,0:T(8,128)} copy(f32[256,8192]{0,1:T(8,128)} %bitcast.78) | data formatting | bytes 16777216 | tf_op jit(solution)/shard_map/reshape | solution.py:51
  548.2 0.0 reduce-scatter.2.cloned.1.call-update
  548.3 0.1 dynamic_slice.12
  548.3 89.2 %reduce-scatter.2.cloned.1.call-done = f32[256,512]{1,0:T(8,128)} async-done(((f32[256,8192]{1,0:T(8,128)}), f32[256,512]{1,0:T(8,128)}) %reduce-scatter.2.cloned.1.call-update) | async-done | bytes 524304 | tf_op jit(solution)/shard_map/reduce_scatter | solution.py:52
  637.6 1.9 multiply_multiply_fusion
  (7 shorter events, 0.0 us)
Async XLA Ops:
  14.9 8.4 %copy-start.1 = (s32[2,16,2]{1,2,0:T(2,128)S(1)}, s32[2,16,2]{1,2,0:T(2,128)}, u32[]{:S(2)}) copy-start(s32[2,16,2]{1,2,0:T(2,128)} %param.10) | copy-start | bytes 772
  14.9 302.2 %all-to-all-start = ((bf16[16,512,1024]{2,1,0:T(8,128)(2,1)}), bf16[16,512,1024]{2,1,0:T(8,128)(2,1)}, u32[]{:S(2)}, u32[]{:S(2)}) async-start(bf16[16,512,1024]{2,1,0:T(8,128)(2,1)} %stack.8), calls=%async_computation | async-start | bytes 33554432 | tf_op jit(solution)/shard_map/all_to_all | solution.py:24
  327.9 10.9 %copy-start = (bf16[2,16,2,128,128]{4,3,2,1,0:T(8,128)(2,1)S(1)}, bf16[2,16,2,128,128]{4,3,2,1,0:T(8,128)(2,1)}, u32[]{:S(2)}) copy-start(bf16[2,16,2,128,128]{4,3,2,1,0:T(8,128)(2,1)} %param.7) | copy-start | bytes 6291460
  372.4 5.4 copy-start.2
  372.4 99.8 %all-to-all-start.1 = ((bf16[2,8,256,1024]{2,3,0,1:T(8,128)(2,1)}), bf16[2,8,256,1024]{2,3,0,1:T(8,128)(2,1)}, u32[]{:S(2)}, u32[]{:S(2)}) async-start(bf16[2,8,256,1024]{2,3,0,1:T(8,128)(2,1)} %pad_maximum_fusion), calls=%async_computation.1 | async-start | bytes 16777216 | tf_op jit(solution)/shard_map/all_to_all | solution.py:42
  377.6 260.0 %reduce-scatter.2.cloned.1.call-start = ((), (), s32[]{:S(2)}) async-start(), calls=%async_computation.3 | async-start | bytes 8912896 | tf_op jit(solution)/shard_map/reduce_scatter | solution.py:52
Sparse Core Ops, SparseCore 0:
  548.4 89.1 reduce-scatter.1
